TPU v7x, 256 devices: a whole 4x4x8 slice. The times are simulated.
256 devices in a mesh: region: 32 (over z, x), cell: 8 (over y, core).
Axes of the slice: x: 4, y: 4, z: 8, core: 2. Of those that a mesh axis runs over, the one named last changes fastest.
Arguments:
- points: float32 [3, 2097152], P(None, ('region', 'cell')), may hold values from -1951 to 1951
- cell_counts: int32 [8192], P(('region', 'cell')), may hold values from 192 to 256
- pair_cells: int32 [2, 106496], P(None, ('region', 'cell')), may hold values from 0 to 31, as said below
- pair_counts: int32 [256], P(('region', 'cell')), may hold values from 32 to 416, as said below
- nugget: float32 [2097152], P(('region', 'cell')), may hold values from 0.1 to 1
- solution: float32 [16, 2097152], P(None, ('region', 'cell')), may hold values from -6 to 6
- residual: float32 [16, 2097152], P(None, ('region', 'cell')), may hold values from -12 to 12
- direction: float32 [16, 2097152], P(None, ('region', 'cell')), may hold values from -12 to 12
- ritz_basis: float32 [32, 2097152], P(None, ('region', 'cell')), may hold values from -1.5 to 1.5
- ritz_image: float32 [32, 2097152], P(None, ('region', 'cell')), may hold values from -0.00390625 to 0.00390625
- inverse_gram: float32 [32, 32], replicated, may hold values from -1 to 1
Outputs:
- solution_out: float32 [16, 2097152], P(None, ('region', 'cell'))
- residual_out: float32 [16, 2097152], P(None, ('region', 'cell'))
- direction_out: float32 [16, 2097152], P(None, ('region', 'cell'))
Inputs may be any that keep to these rules, and one draw needn't show every extreme that they name: `pair_cells`: for each device, column s of its 416 columns is used if s < pair_counts of that device; used columns come first and unused ones hold (0, 0). Row 0 is a cell of that device (0 to 31), row 1 the distance in the cell order to the pair's second cell, 0 to 12; the second cell exists. Each cell is paired with itself exactly once and with the cells that directly follow it up to its last partner, at most 12 of them; used pairs are distinct. Points of two cells that are not paired are more than distance 1 apart. `pair_counts`: some device uses all 416 slots.
All inputs are finite; a program needn't handle non-finite values.
Results may differ from a plain program's by a relative error of at most 0.0025.
Values sent between devices are 32-bit elements; how exact they have to be, the bound alone decides.
No kernel may reach another device: no remote copies, remote signals or barrier semaphores. Data moves between devices by JAX's collectives and lax.ppermute only.
A program may use at most 64 MiB of HBM per device.

v0:
```python
import jax
import jax.numpy as jnp
from jax import lax
from jax.experimental import pallas as pl
from jax.experimental.pallas import tpu as pltpu
from jax.sharding import PartitionSpec as P

PTS = 256
REACH = 12
KF = 48
FAR = 1e18
ROOM = 16.0
AXES = ("region", "cell")
F32 = jnp.float32
BF16 = jnp.bfloat16


def mm(x, y):
    return lax.dot_general(x, y, (((1,), (0,)), ((), ())), preferred_element_type=F32)


def mm_t(x, y):
    return lax.dot_general(x, y, (((1,), (1,)), ((), ())), preferred_element_type=F32)


def high(x):
    return x.astype(BF16).astype(F32)


def split3(x):
    h = high(x)
    m = high(x - h)
    return h, m, high(x - h - m)


def tile_of(scaled_square):
    s = jnp.maximum(scaled_square, 1e-30)
    t = s * lax.rsqrt(s)
    u = jnp.maximum(4.0 - t, 0.0)
    u2 = u * u
    return ((u2 * u2) * (t + 1.0)).astype(BF16)


def cols(block, size=PTS):
    return pl.ds(pl.multiple_of(block * size, size), size)


def with_norm(vec):
    row = lax.broadcasted_iota(jnp.int32, vec.shape, 0)
    return row, jnp.sum(vec * vec, axis=0, keepdims=True)


def weights_side(p):
    row, norm = with_norm(p)
    a = jnp.where(row == 3, norm, -2.0 * p)
    h, m, l = split3(a)
    one_h = jnp.where(row == 3, 1.0, h)
    one_m = jnp.where(row == 3, 1.0, m)
    return jnp.concatenate([h, m, one_h, one_m, l, one_h], axis=0).astype(BF16)


def rows_side(q):
    row, norm = with_norm(q)
    a = jnp.where(row == 3, norm, q)
    h, m, l = split3(a)
    one = jnp.where(row == 3, 1.0, h)
    mid_h = jnp.where(row == 3, h, m)
    return jnp.concatenate([one, one, mid_h, m, one, l], axis=0), norm


def pack(cells, cnt, off, dirs, pts, dc, pc):
    lane1 = lax.broadcasted_iota(jnp.int32, (1, PTS), 1)
    lane128 = lax.broadcasted_iota(jnp.int32, (1, 128), 1)

    def place(c, at):
        off[c] = at
        shift = at % 128
        base = pl.multiple_of((at // 128) * 128, 128)
        live = lane1 < cnt[c]
        dv = jnp.where(live, dirs[:, cols(c)], 0.0)
        pv = jnp.where(live, pts[:, cols(c)], 0.0)
        for ref, val in ((dc, dv), (pc, pv)):
            rows = val.shape[0]
            wide = jnp.concatenate([val, jnp.zeros((rows, 128), F32)], axis=1)
            wide = pltpu.roll(wide, shift, 1)
            old = ref[:rows, pl.ds(base, 128)]
            ref[:rows, pl.ds(base, 128)] = jnp.where(lane128 < shift, old, wide[:, :128])
            ref[:rows, pl.ds(base + 128, 256)] = wide[:, 128:]
        return at + cnt[c]

    return lax.fori_loop(0, cells, place, jnp.int32(0), unroll=8)


def prepare(blocks, pc, end, cen, fs):
    lane1 = lax.broadcasted_iota(jnp.int32, (1, PTS), 1)
    lane128 = lax.broadcasted_iota(jnp.int32, (1, 128), 1)

    def one(j, carry):
        low, top, far = carry
        here = pc[:, cols(j)]
        valid = j * PTS + lane1 < end
        lo = jnp.min(jnp.where(valid, here, FAR), axis=1, keepdims=True)
        hi = jnp.max(jnp.where(valid, here, -FAR), axis=1, keepdims=True)
        centre = jnp.where(lo <= hi, 0.5 * (lo + hi), 0.0)
        cen[pl.ds(pl.multiple_of(j * 8, 8), 8), :] = jnp.broadcast_to(centre, (8, 128))
        feats, norm = rows_side(4.0 * (here - centre))
        fs[cols(j), :] = feats.T.astype(BF16)
        low = jnp.where(lane128 == j, lo, low)
        top = jnp.where(lane128 == j, hi, top)
        return low, top, jnp.maximum(far, jnp.where(valid, norm, 0.0))

    start = (
        jnp.full((8, 128), FAR, F32),
        jnp.full((8, 128), -FAR, F32),
        jnp.zeros((1, PTS), F32),
    )
    low, top, far = lax.fori_loop(0, blocks, one, start, unroll=4 if blocks % 8 else 8)
    cen[pl.ds(blocks * 8, 8), :] = jnp.zeros((8, 128), F32)
    fs[pl.ds(blocks * PTS, PTS), :] = jnp.zeros((PTS, KF), BF16)
    wide = jnp.max(far, axis=1, keepdims=True) > 16.0 * ROOM
    return low, top, jnp.where(wide, 1, 0)


def square(v):
    return jnp.concatenate([v, jnp.zeros((120, 128), F32)], axis=0).T


def near(low_i, top_i, low_j, top_j):
    low_t, top_t = square(low_i), square(top_i)
    gap2 = jnp.zeros((128, 128), F32)
    for k in range(3):
        gap = jnp.maximum(
            low_j[k : k + 1] - top_t[:, k : k + 1], low_t[:, k : k + 1] - top_j[k : k + 1]
        )
        gap = jnp.maximum(gap, 0.0)
        gap2 = gap2 + gap * gap
    return gap2 <= 1.001


def as_rows(last):
    last = jnp.max(last.astype(F32), axis=1, keepdims=True)
    return jnp.broadcast_to(last, (128, 128)).T[:8].astype(jnp.int32)


def to_scalars(values, tab_v, tab_s, sem):
    tab_v[...] = values
    copy = pltpu.make_async_copy(tab_v, tab_s, sem)
    copy.start()
    copy.wait()


def sweep(first, end, begin, stop, spare, spread, side_i, side_j, acc_i, acc_j, bufs):
    pc_i, db_i = side_i
    pc_j, db_j, fs_j, cen_j = side_j
    depth = len(bufs)
    zero = jnp.int32(0)

    def enter(i):
        i = jnp.where(i >= end, spare[0], i)
        return i, jnp.where(i == spare[0], spare[1], begin(i))

    def following(i, j):
        n = j + 1
        over = (n >= stop(i)) | (i == spare[0])
        i2, j2 = enter(i + 1)
        return jnp.where(over, i2, i), jnp.where(over, j2, n)

    def squares(i, j, out):
        c = cen_j[pl.ds(pl.multiple_of(j * 8, 8), 8), :]
        f = weights_side(4.0 * (pc_i[:, cols(i)] - jnp.concatenate([c, c], axis=1)))
        out[...] = mm(fs_j[cols(j), :], f)

    same = db_i is db_j

    def products(i, j, tile):
        other = mm_t(db_i[:, cols(i)], tile)
        if same:
            other = other * jnp.where(j > i, 1.0, 0.0)
        return i, j, mm(db_j[:, cols(j)], tile), other

    def add(i, j, mine, other):
        acc_i[:, cols(i)] += mine
        acc_j[:, cols(j)] += other

    total = lax.fori_loop(first, end, lambda i, n: n + stop(i) - begin(i), zero)
    queue = [enter(jnp.int32(first))]
    for _ in range(depth - 1):
        queue.append(following(*queue[-1]))

    @pl.when(spread == 0)
    def _():
        for k in range(depth - 1):
            squares(*queue[k], bufs[k])

        def turn(units):
            def one(_, carry):
                q = list(carry)
                waiting = None
                for g in range(units):
                    squares(*q[-1], bufs[(g + depth - 1) % depth])
                    done = products(*q[0], tile_of(bufs[g % depth][...]))
                    if waiting is not None:
                        add(*waiting)
                    waiting = done
                    q = q[1:] + [following(*q[-1])]
                add(*waiting)
                return tuple(q)

            return one

        state = lax.fori_loop(0, total // LONG, turn(LONG), tuple(queue))
        left = total - (total // LONG) * LONG
        lax.fori_loop(0, (left + depth - 1) // depth, turn(depth), state)

    @pl.when(spread != 0)
    def _():
        def one(_, carry):
            i, j = carry
            pj = pc_j[:, cols(j)].T
            pi = pc_i[:, cols(i)]
            for h in range(0, PTS, 64):
                s = jnp.zeros((64, PTS), F32)
                for k in range(3):
                    d = 4.0 * (pj[h : h + 64, k : k + 1] - pi[k : k + 1, :])
                    s = s + d * d
                bufs[0][pl.ds(h, 64), :] = s
            add(*products(i, j, tile_of(bufs[0][...])))
            return following(i, j)

        lax.fori_loop(0, total, one, queue[0])


def strips_of(cells, cnt):
    return (lax.fori_loop(0, cells, lambda c, n: n + cnt[c], jnp.int32(0)) + (PTS - 1)) // PTS


def fetch(pairs, sems):
    copies = [pltpu.make_async_copy(src, dst, sems.at[k]) for k, (src, dst) in enumerate(pairs)]
    for copy in copies:
        copy.start()
    return copies


def head_kernel(cells, cnt_h, pts_h, dirs_h, db, pc, fs, cen, box, tab, cnt, pts, dirs, off, dc, sem):
    copies = fetch(((cnt_h, cnt), (pts_h, pts), (dirs_h, dirs)), sem)
    dc[...] = jnp.zeros_like(dc)
    pc[...] = jnp.zeros_like(pc)
    for copy in copies:
        copy.wait()
    own_end = pack(cells, cnt, off, dirs, pts, dc, pc)
    db[...] = dc[...].astype(BF16)
    low, top, spread = prepare(cells, pc, own_end, cen, fs)
    box[0:8, :] = low
    box[8:16, :] = top
    ri = lax.broadcasted_iota(jnp.int32, (128, 128), 0)
    rj = lax.broadcasted_iota(jnp.int32, (128, 128), 1)
    need = near(low, top, low, top) & (rj > ri)
    stop = as_rows(jnp.where(need, rj + 1, ri + 1))
    lane128 = lax.broadcasted_iota(jnp.int32, (1, 128), 1)
    tab[...] = jnp.where(lane128 == 127, spread, stop)


def edge_kernel(cells, halo_cells, cnt, db, pc, box, tab, piece, halo, acc_i, hdb, hfs, hcen, tab_v, *rest):
    *bufs, tab_s, sem = rest
    strips = strips_of(cells, cnt)
    acc_i[...] = jnp.zeros_like(acc_i)
    halo[...] = jnp.zeros_like(halo)
    rhs = hdb.shape[0]
    hdb[:, : halo_cells * PTS] = piece[:rhs, :].astype(BF16)
    hdb[:, halo_cells * PTS :] = jnp.zeros((rhs, PTS), BF16)
    hpc = piece.at[rhs : rhs + 8]
    low, top, spread = prepare(halo_cells, hpc, halo_cells * PTS, hcen, hfs)
    ri = lax.broadcasted_iota(jnp.int32, (128, 128), 0)
    rj = lax.broadcasted_iota(jnp.int32, (128, 128), 1)
    need = near(box[0:8, :], box[8:16, :], low, top) & (rj < halo_cells) & (ri < cells)
    stop = as_rows(jnp.where(need, rj + 1, 0))
    lane128 = lax.broadcasted_iota(jnp.int32, (1, 128), 1)
    first = jnp.min(jnp.where(need, ri, 127).astype(F32), axis=(0, 1), keepdims=True)
    stop = jnp.where(lane128 == 126, first.astype(jnp.int32), stop)
    wide = jnp.where((tab[...] != 0) & (lane128 == 127), 1, 0)
    to_scalars(jnp.where(lane128 == 127, spread + wide, stop), tab_v, tab_s, sem)
    sweep(
        jnp.minimum(tab_s[0, 126], strips), strips, lambda i: jnp.int32(0),
        lambda i: jnp.maximum(tab_s[0, i], 1), (cells, halo_cells), tab_s[0, 127],
        (pc, db), (hpc, hdb, hfs, hcen), acc_i, halo, bufs,
    )
    halo[:, : halo_cells * PTS] = halo[:, : halo_cells * PTS] * (1.0 / 256.0)


def tail_kernel(cells, cnt, db, pc, fs, cen, tab, acc_e, own, off, acc_i, acc_j, *rest):
    bufs = rest
    lane1 = lax.broadcasted_iota(jnp.int32, (1, PTS), 1)
    acc_i[...] = acc_e[...]
    acc_j[...] = jnp.zeros_like(acc_j)

    def place(c, at):
        off[c] = at
        return at + cnt[c]

    end = lax.fori_loop(0, cells, place, jnp.int32(0))
    strips = (end + (PTS - 1)) // PTS
    side = (pc, db, fs, cen)
    sweep(
        0, strips, lambda i: i, lambda i: tab[0, i], (cells, cells), tab[0, 127],
        side[:2], side, acc_i, acc_j, bufs,
    )

    def take(c, _):
        at = off[c]
        base = pl.multiple_of((at // 128) * 128, 128)
        both = acc_i[:, pl.ds(base, 384)] + acc_j[:, pl.ds(base, 384)]
        back = pltpu.roll(both, 384 - at % 128, 1)[:, :PTS] * (1.0 / 256.0)
        own[:, cols(c)] = jnp.where(lane1 < cnt[c], back, 0.0)
        return 0

    lax.fori_loop(0, cells, take, 0, unroll=4)


def piece_kernel(cells, cnt_h, pts_h, dirs_h, piece, cnt, pts, dirs, sem):
    rhs = dirs.shape[0]
    span = pl.ds(0, cells * PTS)
    copies = fetch(((cnt_h, cnt), (pts_h.at[:, span], pts), (dirs_h.at[:, span], dirs)), sem)
    lane1 = lax.broadcasted_iota(jnp.int32, (1, PTS), 1)
    piece[rhs:, :] = jnp.zeros_like(piece[rhs:, :])
    for copy in copies:
        copy.wait()
    for c in range(cells):
        at = slice(c * PTS, (c + 1) * PTS)
        live = lane1 < cnt[c]
        piece[:rhs, at] = jnp.where(live, dirs[:, at], 0.0)
        piece[rhs : rhs + 3, at] = jnp.where(live, pts[:, at], pts[:, c * PTS : c * PTS + 1])


VM = pl.BlockSpec(memory_space=pltpu.VMEM)
SM = pl.BlockSpec(memory_space=pltpu.SMEM)
HB = pl.BlockSpec(memory_space=pltpu.MemorySpace.HBM)
LONG = 16
DEPTH = 4


def params(mib):
    return pltpu.CompilerParams(vmem_limit_bytes=mib << 20)


def buffers():
    return [pltpu.VMEM((PTS, PTS), F32)] * DEPTH


def cost(units):
    return pl.CostEstimate(flops=units * 60_000_000, bytes_accessed=4_000_000, transcendentals=units * 65536)


def pair_products(counts, points, direction):
    cells = counts.shape[0]
    rhs = direction.shape[0]
    width = min(cells, REACH)
    blocks = cells + 1
    wide = blocks * PTS + 256
    shape = jax.ShapeDtypeStruct

    piece = pl.pallas_call(
        lambda *refs: piece_kernel(width, *refs),
        name="piece",
        out_shape=shape((rhs + 8, width * PTS), F32),
        in_specs=[HB] * 3,
        out_specs=VM,
        scratch_shapes=[
            pltpu.SMEM((cells,), jnp.int32),
            pltpu.VMEM((3, width * PTS), F32),
            pltpu.VMEM((rhs, width * PTS), F32),
            pltpu.SemaphoreType.DMA((3,)),
        ],
        compiler_params=params(8),
    )(counts, points, direction)
    piece = passed_along(piece, -1)
    db, pc, fs, cen, box, tab = pl.pallas_call(
        lambda *refs: head_kernel(cells, *refs),
        name="head",
        out_shape=[
            shape((rhs, wide), BF16),
            shape((8, wide), F32),
            shape((blocks * PTS, KF), BF16),
            shape((blocks * 8, 128), F32),
            shape((16, 128), F32),
            shape((8, 128), jnp.int32),
        ],
        in_specs=[HB] * 3,
        out_specs=[VM] * 6,
        scratch_shapes=[
            pltpu.SMEM((cells,), jnp.int32),
            pltpu.VMEM(points.shape, F32),
            pltpu.VMEM(direction.shape, F32),
            pltpu.SMEM((cells,), jnp.int32),
            pltpu.VMEM((rhs, wide), F32),
            pltpu.SemaphoreType.DMA((3,)),
        ],
        compiler_params=params(12),
        cost_estimate=cost(100),
    )(counts, points, direction)
    halo, acc_e = pl.pallas_call(
        lambda *refs: edge_kernel(cells, width, *refs),
        name="edge",
        out_shape=[shape((rhs, (width + 1) * PTS), F32), shape((rhs, wide), F32)],
        in_specs=[SM] + [VM] * 5,
        out_specs=[VM] * 2,
        scratch_shapes=[
            pltpu.VMEM((rhs, (width + 1) * PTS), BF16),
            pltpu.VMEM(((width + 1) * PTS, KF), BF16),
            pltpu.VMEM(((width + 1) * 8, 128), F32),
            pltpu.VMEM((8, 128), jnp.int32),
        ]
        + buffers()
        + [pltpu.SMEM((8, 128), jnp.int32), pltpu.SemaphoreType.DMA],
        compiler_params=params(12),
        cost_estimate=cost(70),
    )(counts, db, pc, box, tab, piece)
    back = passed_along(halo, 1)
    own = pl.pallas_call(
        lambda *refs: tail_kernel(cells, *refs),
        name="tail",
        out_shape=shape((rhs, cells * PTS), F32),
        in_specs=[SM] + [VM] * 4 + [SM, VM],
        out_specs=VM,
        scratch_shapes=[
            pltpu.SMEM((cells,), jnp.int32),
            pltpu.VMEM((rhs, wide), F32),
            pltpu.VMEM((rhs, wide), F32),
        ]
        + buffers(),
        compiler_params=params(12),
        cost_estimate=cost(180),
    )(counts, db, pc, fs, cen, tab, acc_e)
    return own, back


def sums_kernel(cnt, own, back, nug, dirs, res, ritz, image, sums):
    cells = own.shape[1] // PTS
    halo_cells = back.shape[1] // PTS - 1
    lane1 = lax.broadcasted_iota(jnp.int32, (1, PTS), 1)

    def of_cell(c, part, extra):
        live = lane1 < cnt[c]
        d = jnp.where(live, dirs[:, cols(c)], 0.0)
        r = jnp.where(live, res[:, cols(c)], 0.0)
        k = own[:, cols(c)]
        if extra:
            k = k + back[:, cols(c)]
        im = jnp.where(live, nug[:, cols(c)] * d + k, 0.0)
        image[:, cols(c)] = im
        dk, rr, ri, ii, prod = part
        both = jnp.concatenate([r, im], axis=0)
        bh = high(both)
        z = ritz[:, cols(c)]
        zh = high(z)
        left = jnp.concatenate([bh, both - bh], axis=0).astype(BF16)
        right = jnp.concatenate([zh, z - zh], axis=0).astype(BF16)
        return dk + d * im, rr + r * r, ri + r * im, ii + im * im, prod + mm_t(left, right)

    rhs = own.shape[0]
    zero = jnp.zeros((rhs, PTS), F32)
    part = (zero, zero, zero, zero, jnp.zeros((4 * rhs, 2 * ritz.shape[0]), F32))
    part = lax.fori_loop(0, halo_cells, lambda c, p: of_cell(c, p, True), part, unroll=4)
    part = lax.fori_loop(halo_cells, cells, lambda c, p: of_cell(c, p, False), part, unroll=4)
    dots = [jnp.sum(p, axis=1, keepdims=True) for p in part[:4]]
    prod = part[4]
    n = ritz.shape[0]
    h = 2 * rhs
    prod = prod[:h, :n] + prod[:h, n:] + prod[h:, :n]
    sums[...] = jnp.zeros_like(sums)
    sums[:, :n] = prod[:rhs]
    sums[:, n : 2 * n] = prod[rhs:]
    for k in range(4):
        sums[:, 2 * n + k : 2 * n + k + 1] = dots[k]


def local_sums(counts, own, back, nugget, direction, residual, ritz_image):
    return pl.pallas_call(
        sums_kernel,
        name="sums",
        out_shape=[
            jax.ShapeDtypeStruct(own.shape, F32),
            jax.ShapeDtypeStruct((own.shape[0], 128), F32),
        ],
        in_specs=[SM] + [VM] * 6,
        out_specs=[VM, VM],
        compiler_params=params(12),
    )(counts, own, back, nugget, direction, residual, ritz_image)


def finish_kernel(
    cnt, sums, gram, image, dirs, res, sol, basis, sol_h, res_h, dir_h, sol_out, res_out, dir_out, sem
):
    cells = image.shape[1] // PTS
    n = gram.shape[0]
    lane1 = lax.broadcasted_iota(jnp.int32, (1, PTS), 1)
    curvature, rr, ri, ii = (sums[:, 2 * n + k : 2 * n + k + 1] for k in range(4))
    step = rr / curvature
    growth = (rr + step * (step * ii - 2.0 * ri)) / rr
    projected = sums[:, :n] - step * sums[:, n : 2 * n]
    coef = lax.dot_general(
        projected,
        gram[...],
        (((1,), (1,)), ((), ())),
        precision=lax.Precision.HIGHEST,
        preferred_element_type=F32,
    )
    ch = high(coef)
    left = jnp.concatenate([ch, ch, coef - ch], axis=1).astype(BF16)

    def of_cell(c, _):
        live = lane1 < cnt[c]
        d = jnp.where(live, dirs[:, cols(c)], 0.0)
        r = jnp.where(live, res[:, cols(c)], 0.0)
        s = jnp.where(live, sol[:, cols(c)], 0.0)
        b = basis[:, cols(c)]
        bh = high(b)
        right = jnp.concatenate([bh, b - bh, bh], axis=0).astype(BF16)
        new = r - step * image[:, cols(c)]
        sol_out[:, cols(c)] = s + step * d
        res_out[:, cols(c)] = new
        dir_out[:, cols(c)] = jnp.where(live, growth * d + new - mm(left, right), 0.0)
        return 0

    pieces = 4
    many = cells // pieces
    copies = []
    for k in range(pieces):
        lax.fori_loop(k * many, (k + 1) * many, of_cell, 0, unroll=4)
        at = pl.ds(k * many * PTS, many * PTS)
        for n, (src, dst) in enumerate(((sol_out, sol_h), (res_out, res_h), (dir_out, dir_h))):
            copies.append(pltpu.make_async_copy(src.at[:, at], dst.at[:, at], sem.at[3 * k + n]))
            copies[-1].start()
    for copy in copies:
        copy.wait()


def finish(counts, sums, gram, image, direction, residual, solution, basis):
    return pl.pallas_call(
        finish_kernel,
        name="finish",
        out_shape=[jax.ShapeDtypeStruct(image.shape, F32)] * 3,
        in_specs=[SM] + [VM] * 7,
        out_specs=[HB] * 3,
        scratch_shapes=[pltpu.VMEM(image.shape, F32)] * 3 + [pltpu.SemaphoreType.DMA((12,))],
        compiler_params=params(12),
    )(counts, sums, gram, image, direction, residual, solution, basis)


def passed_along(array, by):
    length = lax.axis_size(AXES)
    pairs = [(i, i + by) for i in range(length) if 0 <= i + by < length]
    return lax.ppermute(array, AXES, pairs)


def summed(array):
    for axis in ("cell", "region"):
        copies = jnp.broadcast_to(array[None], (lax.axis_size(axis),) + array.shape)
        array = jnp.sum(lax.all_to_all(copies, axis, 0, 0), axis=0)
    return array


def local(
    points,
    cell_counts,
    pair_cells,
    pair_counts,
    nugget,
    solution,
    residual,
    direction,
    ritz_basis,
    ritz_image,
    inverse_gram,
):
    own, back = pair_products(cell_counts, points, direction)
    image, sums = local_sums(
        cell_counts, own, back, nugget.reshape(1, -1), direction, residual, ritz_image
    )
    return tuple(
        finish(
            cell_counts,
            summed(sums),
            inverse_gram,
            image,
            direction,
            residual,
            solution,
            ritz_basis,
        )
    )


def solution(mesh):
    split = P(None, AXES)
    line = P(AXES)
    in_specs = (split, line, split, line, line, split, split, split, split, split, P())
    return jax.shard_map(
        local, mesh=mesh, in_specs=in_specs, out_specs=(split,) * 3, check_vma=False
    )
```

profile of v0, /device:TPU:32, one launch (start us, length us, event | category | flops | bytes accessed | tf_op | source)
XLA Modules:
  0.0 95.3 jit_solution(2065288590980772154)
XLA Ops:
  0.6 0.0 copy-start
  0.6 1.0 %copy-done = f32[16,8192]{1,0:T(8,128)S(1)} copy-done((f32[16,8192]{1,0:T(8,128)S(1)}, f32[16,8192]{1,0:T(8,128)}, u32[]{:S(2)}) %copy-start) | copy-done | bytes 524312
  1.7 0.0 copy-start.7
  1.7 0.9 copy-done.7
  2.6 0.0 copy-start.11
  2.6 0.7 copy-done.11
  3.2 0.7 piece.1
  3.9 6.1 %collective-permute-start = (f32[24,3072]{1,0:T(8,128)S(1)}, f32[24,3072]{1,0:T(8,128)S(1)}, u32[]{:S(2)}, u32[]{:S(2)}) collective-permute-start(f32[24,3072]{1,0:T(8,128)S(1)} %piece.1), channel_id=1, source_target_pairs={{1,0},{2,1},{3,2},{4,3},{5,4},{6,5},{7,6},{8,7},{9,8},{10,9},{11,1... | collective-permute-start | bytes 884744 | tf_op jit(solution)/shard_map/ppermute | solution.py:552
  10.0 0.0 copy-start.1
  10.0 1.0 %copy-done.1 = f32[16,8192]{1,0:T(8,128)S(1)} copy-done((f32[16,8192]{1,0:T(8,128)S(1)}, f32[16,8192]{1,0:T(8,128)}, u32[]{:S(2)}) %copy-start.1) | copy-done | bytes 524312
  11.0 0.0 copy-start.8
  11.1 0.9 copy-done.8
  12.0 0.0 copy-start.12
  12.0 0.7 copy-done.12
  12.6 3.0 %head.1 = (bf16[16,8704]{1,0:T(8,128)(2,1)S(1)}, f32[8,8704]{1,0:T(8,128)S(1)}, bf16[8448,48]{1,0:T(8,128)(2,1)S(1)}, f32[264,128]{1,0:T(8,128)S(1)}, f32[16,128]{1,0:T(8,128)S(1)}, /*index=5*/s32[8,128]{1,0:T(8,128)S(1)}) custom-call(s32[32]{0:T(128)S(1)} %copy-done.12, f32[3,8192]{1,0:T(4,128)S(1)} %copy-done.8, f32[16,8192]{1,0:T(8,128)S(1)} %copy-done.1), custom_call_target="tpu_custom_call" | custom-call | flops 6000000000 | bytes 4000000 | tf_op jit(solution)/shard_map/head/pallas_call | solution.py:376
  15.6 0.0 collective-permute-done.refs_5_
  15.6 10.0 %edge.1 = (f32[16,3328]{1,0:T(8,128)S(1)}, f32[16,8704]{1,0:T(8,128)S(1)}) custom-call(s32[32]{0:T(128)S(1)} %copy-done.12, bf16[16,8704]{1,0:T(8,128)(2,1)S(1)} %get-tuple-element.13.refs_1_, f32[8,8704]{1,0:T(8,128)S(1)} %get-tuple-element.14.refs_2_, f32[16,128]{1,0:T(8,128)S(1)} %get-tuple-element.18.refs_3_, ...), custom_call_target="tpu_custom_call" | custom-call | flops 4200000000 | bytes 4000000 | tf_op jit(solution)/shard_map/edge/pallas_call | solution.py:400
  25.6 1.9 %collective-permute-start.1 = (f32[16,3328]{1,0:T(8,128)S(1)}, f32[16,3328]{1,0:T(8,128)S(1)}, u32[]{:S(2)}, u32[]{:S(2)}) collective-permute-start(f32[16,3328]{1,0:T(8,128)S(1)} %get-tuple-element.20), channel_id=1, source_target_pairs={{0,1},{1,2},{2,3},{3,4},{4,5},{5,6},{6,7},{7,8},{8,9},{9,10},{10,1... | collective-permute-start | bytes 638984 | tf_op jit(solution)/shard_map/ppermute | solution.py:552
  27.5 0.0 copy-start.2
  27.5 0.0 copy-start.3
  27.6 0.0 copy-start.4
  27.6 0.0 copy-start.9
  27.6 29.4 %tail.1.own = f32[16,8192]{1,0:T(8,128)S(1)} custom-call(s32[32]{0:T(128)S(1)} %copy-done.12, bf16[16,8704]{1,0:T(8,128)(2,1)S(1)} %get-tuple-element.13.refs_1_, f32[8,8704]{1,0:T(8,128)S(1)} %get-tuple-element.14.refs_2_, bf16[8448,48]{1,0:T(8,128)(2,1)S(1)} %get-tuple-element.15.refs_3_, f32[264,128]{1,0:T(8,128)S(1)} %get-tuple-element.16.refs_4_, ...), custom_call_target="tpu_custom_call" | custom-call | flops 10800000000 | bytes 4000000 | tf_op jit(solution)/shard_map/tail/pallas_call | solution.py:418
  56.9 0.0 copy-start.5
  56.9 0.0 copy-start.6
  57.0 0.0 copy-start.10
  57.0 0.0 copy-start.13
  57.0 0.0 collective-permute-done.1.back
  57.0 0.0 copy-done.2
  57.0 0.0 copy-done.3
  57.0 0.0 copy-done.4
  57.0 0.0 copy-done.9
  57.0 2.2 %sums.1 = (f32[16,8192]{1,0:T(8,128)S(1)}, f32[16,128]{1,0:T(8,128)S(1)}) custom-call(s32[32]{0:T(128)S(1)} %copy-done.12, f32[16,8192]{1,0:T(8,128)S(1)} %tail.1.own, f32[16,3328]{1,0:T(8,128)S(1)} %collective-permute-done.1.back, f32[1,8192]{1,0:T(1,128)S(1)} %bitcast.1, f32[16,8192]{1,0:T(8,128)S(1)} %copy-done.2, f32[16,8192]{1,0:T(8,128)S(1)} %copy-done.3, ...), custom_call_target="tpu_custom_call" | custom-call | tf_op jit(solution)/shard_map/sums/pallas_call | solution.py:477
  59.3 8.0 %all_to_all.10 = f32[8,16,128]{2,1,0:T(8,128)S(1)} all-to-all(f32[8,16,128]{2,1,0:T(8,128)S(1)} %broadcast_in_dim.4), channel_id=1, replica_groups=mesh['region'=32,'cell'=8] {'cell'}, dimensions={0} | all-to-all | bytes 131072 | tf_op jit(solution)/shard_map/all_to_all | solution.py:558
  67.3 24.9 %all_to_all.11 = f32[32,16,128]{2,1,0:T(8,128)S(1)} all-to-all(f32[32,16,128]{2,1,0:T(8,128)S(1)} %broadcast_in_dim.5), channel_id=1, replica_groups=mesh['region'=32,'cell'=8] {'region'}, dimensions={0} | all-to-all | bytes 524288 | tf_op jit(solution)/shard_map/all_to_all | solution.py:558
  92.3 0.0 copy-done.5
  92.3 0.0 copy-done.6
  92.4 0.0 copy-done.10
  92.4 0.0 copy-done.13
  92.4 2.9 %finish.1 = (f32[16,8192]{1,0:T(8,128)}, f32[16,8192]{1,0:T(8,128)}, f32[16,8192]{1,0:T(8,128)}) custom-call(s32[32]{0:T(128)S(1)} %copy-done.13, f32[16,128]{1,0:T(8,128)S(1)} %reduce_sum.19.sums, f32[32,32]{1,0:T(8,128)S(1)} %copy-done.10, f32[16,8192]{1,0:T(8,128)S(1)} %get-tuple-element.22.image, f32[16,8192]{1,0:T(8,128)S(1)} %copy-done.2, ...), custom_call_target="tpu_custom_call" | custom-call | tf_op jit(solution)/shard_map/finish/pallas_call | solution.py:538
  (4 shorter events, 0.1 us)
Async XLA Ops:
  0.6 1.0 %copy-start = (f32[16,8192]{1,0:T(8,128)S(1)}, f32[16,8192]{1,0:T(8,128)}, u32[]{:S(2)}) copy-start(f32[16,8192]{1,0:T(8,128)} %dirs.3) | copy-start | bytes 1572868
  1.7 0.9 copy-start.7
  2.6 0.7 copy-start.11
  3.9 11.7 %collective-permute-start = (f32[24,3072]{1,0:T(8,128)S(1)}, f32[24,3072]{1,0:T(8,128)S(1)}, u32[]{:S(2)}, u32[]{:S(2)}) collective-permute-start(f32[24,3072]{1,0:T(8,128)S(1)} %piece.1), channel_id=1, source_target_pairs={{1,0},{2,1},{3,2},{4,3},{5,4},{6,5},{7,6},{8,7},{9,8},{10,9},{11,1... | collective-permute-start | bytes 884744 | tf_op jit(solution)/shard_map/ppermute | solution.py:552
  10.0 1.0 %copy-start.1 = (f32[16,8192]{1,0:T(8,128)S(1)}, f32[16,8192]{1,0:T(8,128)}, u32[]{:S(2)}) copy-start(f32[16,8192]{1,0:T(8,128)} %dirs.3) | copy-start | bytes 1572868
  11.0 0.9 copy-start.8
  12.0 0.7 copy-start.12
  25.6 31.4 %collective-permute-start.1 = (f32[16,3328]{1,0:T(8,128)S(1)}, f32[16,3328]{1,0:T(8,128)S(1)}, u32[]{:S(2)}, u32[]{:S(2)}) collective-permute-start(f32[16,3328]{1,0:T(8,128)S(1)} %get-tuple-element.20), channel_id=1, source_target_pairs={{0,1},{1,2},{2,3},{3,4},{4,5},{5,6},{6,7},{7,8},{8,9},{9,10},{10,1... | collective-permute-start | bytes 638984 | tf_op jit(solution)/shard_map/ppermute | solution.py:552
  27.5 29.5 %copy-start.2 = (f32[16,8192]{1,0:T(8,128)S(1)}, f32[16,8192]{1,0:T(8,128)}, u32[]{:S(2)}) copy-start(f32[16,8192]{1,0:T(8,128)} %dirs.3) | copy-start | bytes 1572868
  27.5 29.5 %copy-start.3 = (f32[16,8192]{1,0:T(8,128)S(1)}, f32[16,8192]{1,0:T(8,128)}, u32[]{:S(2)}) copy-start(f32[16,8192]{1,0:T(8,128)} %res.3) | copy-start | bytes 1572868
  27.6 29.5 %copy-start.4 = (f32[32,8192]{1,0:T(8,128)S(1)}, f32[32,8192]{1,0:T(8,128)}, u32[]{:S(2)}) copy-start(f32[32,8192]{1,0:T(8,128)} %ritz.1) | copy-start | bytes 3145732
  27.6 29.5 %copy-start.9 = (f32[8192]{0:T(1024)S(1)}, f32[8192]{0:T(1024)}, u32[]{:S(2)}) copy-start(f32[8192]{0:T(1024)} %param.13) | copy-start | bytes 98308
  56.9 35.4 %copy-start.5 = (f32[32,8192]{1,0:T(8,128)S(1)}, f32[32,8192]{1,0:T(8,128)}, u32[]{:S(2)}) copy-start(f32[32,8192]{1,0:T(8,128)} %basis.1) | copy-start | bytes 3145732
  56.9 35.4 %copy-start.6 = (f32[16,8192]{1,0:T(8,128)S(1)}, f32[16,8192]{1,0:T(8,128)}, u32[]{:S(2)}) copy-start(f32[16,8192]{1,0:T(8,128)} %sol.1) | copy-start | bytes 1572868
  57.0 35.4 %copy-start.10 = (f32[32,32]{1,0:T(8,128)S(1)}, f32[32,32]{1,0:T(8,128)}, u32[]{:S(2)}) copy-start(f32[32,32]{1,0:T(8,128)} %gram.1) | copy-start | bytes 12292
  57.0 35.4 %copy-start.13 = (s32[32]{0:T(128)S(1)}, s32[32]{0:T(128)}, u32[]{:S(2)}) copy-start(s32[32]{0:T(128)} %cnt.3) | copy-start | bytes 388
where the time goes:
time: 94.4 us; the launch traced here: 95.3 us
  Pallas kernels  48.1 us (51%)
  blocking collectives  32.9 us (35%)
  starting transfers between devices  8.02 us (8%)
  local copies, waits for them, and re-layouts  5.29 us (6%)
    all_to_all x2, blocking collectives, summed(): array = jnp.sum(lax.all_to_all(copies, axis, 0, 0), axis=0)  32.9 us
    pallas_call x1, Pallas kernels, pair_products(): pl.pallas_call(lambda *refs: tail_kernel(cells, *refs), name='tail', out_...  29.4 us
    pallas_call x1, Pallas kernels, pair_products(): pl.pallas_call(lambda *refs: edge_kernel(cells, width, *refs), name='edge...  9.99 us
    ppermute x2, starting transfers between devices, passed_along(): return lax.ppermute(array, AXES, pairs)  8.02 us
    unnamed x28, local copies, waits for them, and re-layouts  5.24 us
    pallas_call x1, Pallas kernels, pair_products(): pl.pallas_call(lambda *refs: head_kernel(cells, *refs), name='head', out_...  2.98 us
    pallas_call x1, Pallas kernels, finish(): pl.pallas_call(finish_kernel, name='finish', out_shape=[jax.ShapeDtypeStr...  2.93 us
    pallas_call x1, Pallas kernels, local_sums(): pl.pallas_call(sums_kernel, name='sums', out_shape=[jax.ShapeDtypeStruct(...  2.24 us
  transfers between devices with their start and end apart: 2, of which 0 were waited for; matrix products, arithmetic and copies ran while one was open for 0% of the time, Pallas kernels for 34%

commit v1 on v0

--- a/solution.py
+++ b/solution.py
@@ -358,6 +358,7 @@
     wide = blocks * PTS + 256
     shape = jax.ShapeDtypeStruct
 
+    held = [pltpu.with_memory_space_constraint(x, pltpu.MemorySpace.HBM) for x in (counts, points, direction)]
     piece = pl.pallas_call(
         lambda *refs: piece_kernel(width, *refs),
         name="piece",
@@ -371,7 +372,7 @@
             pltpu.SemaphoreType.DMA((3,)),
         ],
         compiler_params=params(8),
-    )(counts, points, direction)
+    )(*held)
     piece = passed_along(piece, -1)
     db, pc, fs, cen, box, tab = pl.pallas_call(
         lambda *refs: head_kernel(cells, *refs),
@@ -396,7 +397,7 @@
         ],
         compiler_params=params(12),
         cost_estimate=cost(100),
-    )(counts, points, direction)
+    )(*held)
     halo, acc_e = pl.pallas_call(
         lambda *refs: edge_kernel(cells, width, *refs),
         name="edge",
@@ -459,8 +460,8 @@
     rhs = own.shape[0]
     zero = jnp.zeros((rhs, PTS), F32)
     part = (zero, zero, zero, zero, jnp.zeros((4 * rhs, 2 * ritz.shape[0]), F32))
-    part = lax.fori_loop(0, halo_cells, lambda c, p: of_cell(c, p, True), part, unroll=4)
-    part = lax.fori_loop(halo_cells, cells, lambda c, p: of_cell(c, p, False), part, unroll=4)
+    part = lax.fori_loop(0, halo_cells, lambda c, p: of_cell(c, p, True), part, unroll=6)
+    part = lax.fori_loop(halo_cells, cells, lambda c, p: of_cell(c, p, False), part, unroll=5)
     dots = [jnp.sum(p, axis=1, keepdims=True) for p in part[:4]]
     prod = part[4]
     n = ritz.shape[0]
@@ -497,12 +498,12 @@
     step = rr / curvature
     growth = (rr + step * (step * ii - 2.0 * ri)) / rr
     projected = sums[:, :n] - step * sums[:, n : 2 * n]
-    coef = lax.dot_general(
-        projected,
-        gram[...],
-        (((1,), (1,)), ((), ())),
-        precision=lax.Precision.HIGHEST,
-        preferred_element_type=F32,
+    ph = high(projected)
+    g = gram[...]
+    gh = high(g)
+    coef = mm_t(
+        jnp.concatenate([ph, ph, projected - ph], axis=1).astype(BF16),
+        jnp.concatenate([gh, g - gh, gh], axis=1).astype(BF16),
     )
     ch = high(coef)
     left = jnp.concatenate([ch, ch, coef - ch], axis=1).astype(BF16)
@@ -525,7 +526,7 @@
     many = cells // pieces
     copies = []
     for k in range(pieces):
-        lax.fori_loop(k * many, (k + 1) * many, of_cell, 0, unroll=4)
+        lax.fori_loop(k * many, (k + 1) * many, of_cell, 0, unroll=8)
         at = pl.ds(k * many * PTS, many * PTS)
         for n, (src, dst) in enumerate(((sol_out, sol_h), (res_out, res_h), (dir_out, dir_h))):
             copies.append(pltpu.make_async_copy(src.at[:, at], dst.at[:, at], sem.at[3 * k + n]))
@@ -552,10 +553,19 @@
     return lax.ppermute(array, AXES, pairs)
 
 
+def groups_of(length, bits):
+    others = [i for i in range(length) if not any(i >> b & 1 for b in bits)]
+    spread = [sum((m >> k & 1) << b for k, b in enumerate(bits)) for m in range(1 << len(bits))]
+    return [[i + s for s in spread] for i in others]
+
+
 def summed(array):
-    for axis in ("cell", "region"):
-        copies = jnp.broadcast_to(array[None], (lax.axis_size(axis),) + array.shape)
-        array = jnp.sum(lax.all_to_all(copies, axis, 0, 0), axis=0)
+    length = lax.axis_size(AXES)
+    array = array + lax.ppermute(array, AXES, [(i, i ^ 1) for i in range(length)])
+    for bits in ((1, 2, 3, 4), (5, 6, 7)):
+        copies = jnp.broadcast_to(array[None], (1 << len(bits),) + array.shape)
+        parts = lax.all_to_all(copies, AXES, 0, 0, axis_index_groups=groups_of(length, bits))
+        array = jnp.sum(parts, axis=0)
     return array
 
 

time: 94.4 us -> 87.1 us (0.923); the launches traced: 95.3 us -> 86.3 us
  blocking collectives: 32.9 us -> 26.7 us
  local copies, waits for them, and re-layouts: 5.29 us -> 0.07 us
  waiting for transfers between devices: 0.01 us -> 1.82 us
    all_to_all x2, blocking collectives: 32.9 us -> 26.7 us  [summed(): lax.all_to_all(copies, AXES, 0, 0, axis_index_groups=groups_of(length, bi...]
    unnamed x28 -> x16, local copies, waits for them, and re-layouts: 5.24 us -> 0.05 us
    ppermute x0 -> x1, waiting for transfers between devices: none -> 1.16 us  [summed(): lax.ppermute(array, AXES, [(i, i ^ 1) for i in range(length)])]
  transfers between devices with their start and end apart: 2 -> 3, of which waited for: 0 -> 2; matrix products, arithmetic and copies ran while one was open for 0% -> 0% of each run, Pallas kernels for 34% -> 39%
where the time goes in v1:
time: 87.1 us; the launch traced here: 86.3 us
  Pallas kernels  48.8 us (56%)
  blocking collectives  26.7 us (31%)
  starting transfers between devices  8.1 us (9%)
  waiting for transfers between devices  1.82 us (2%)
    pallas_call x1, Pallas kernels, pair_products(): pl.pallas_call(lambda *refs: tail_kernel(cells, *refs), name='tail', out_...  29.8 us
    all_to_all x2, blocking collectives, summed(): lax.all_to_all(copies, AXES, 0, 0, axis_index_groups=groups_of(length, bi...  26.7 us
    pallas_call x1, Pallas kernels, pair_products(): pl.pallas_call(lambda *refs: edge_kernel(cells, width, *refs), name='edge...  9.98 us
    ppermute x2, starting transfers between devices, passed_along(): return lax.ppermute(array, AXES, pairs)  8.02 us
    pallas_call x1, Pallas kernels, pair_products(): pl.pallas_call(lambda *refs: head_kernel(cells, *refs), name='head', out_...  3.55 us
    pallas_call x1, Pallas kernels, finish(): pl.pallas_call(finish_kernel, name='finish', out_shape=[jax.ShapeDtypeStr...  2.34 us
    pallas_call x1, Pallas kernels, local_sums(): pl.pallas_call(sums_kernel, name='sums', out_shape=[jax.ShapeDtypeStruct(...  1.98 us
  transfers between devices with their start and end apart: 3, of which 2 were waited for; matrix products, arithmetic and copies ran while one was open for 0% of the time, Pallas kernels for 39%

profile of v1, /device:TPU:32, one launch (start us, length us, event | category | flops | bytes accessed | tf_op | source)
XLA Modules:
  0.0 86.3 jit_solution(7440733014451275729)
XLA Ops:
  0.6 1.1 %piece.1 = f32[24,3072]{1,0:T(8,128)S(1)} custom-call(s32[32]{0:T(128)} %cnt.3, f32[3,8192]{1,0:T(4,128)} %refs_1_.3, f32[16,8192]{1,0:T(8,128)} %dirs.3), custom_call_target="tpu_custom_call" | custom-call | tf_op jit(solution)/shard_map/piece/pallas_call | solution.py:362
  1.7 0.0 copy-start.7
  1.7 6.1 %collective-permute-start = (f32[24,3072]{1,0:T(8,128)S(1)}, f32[24,3072]{1,0:T(8,128)S(1)}, u32[]{:S(2)}, u32[]{:S(2)}) collective-permute-start(f32[24,3072]{1,0:T(8,128)S(1)} %piece.1), channel_id=1, source_target_pairs={{1,0},{2,1},{3,2},{4,3},{5,4},{6,5},{7,6},{8,7},{9,8},{10,9},{11,1... | collective-permute-start | bytes 884744 | tf_op jit(solution)/shard_map/ppermute | solution.py:553
  7.8 3.6 %head.1 = (bf16[16,8704]{1,0:T(8,128)(2,1)S(1)}, f32[8,8704]{1,0:T(8,128)S(1)}, bf16[8448,48]{1,0:T(8,128)(2,1)S(1)}, f32[264,128]{1,0:T(8,128)S(1)}, f32[16,128]{1,0:T(8,128)S(1)}, /*index=5*/s32[8,128]{1,0:T(8,128)S(1)}) custom-call(s32[32]{0:T(128)} %cnt.3, f32[3,8192]{1,0:T(4,128)} %refs_1_.3, f32[16,8192]{1,0:T(8,128)} %dirs.3), custom_call_target="tpu_custom_call" | custom-call | flops 6000000000 | bytes 4000000 | tf_op jit(solution)/shard_map/head/pallas_call | solution.py:377
  11.4 0.7 collective-permute-done.refs_5_
  12.0 0.0 copy-done.7
  12.1 10.0 %edge.1 = (f32[16,3328]{1,0:T(8,128)S(1)}, f32[16,8704]{1,0:T(8,128)S(1)}) custom-call(s32[32]{0:T(128)S(1)} %copy-done.7, bf16[16,8704]{1,0:T(8,128)(2,1)S(1)} %get-tuple-element.13.refs_1_, f32[8,8704]{1,0:T(8,128)S(1)} %get-tuple-element.14.refs_2_, f32[16,128]{1,0:T(8,128)S(1)} %get-tuple-element.18.refs_3_, ...), custom_call_target="tpu_custom_call" | custom-call | flops 4200000000 | bytes 4000000 | tf_op jit(solution)/shard_map/edge/pallas_call | solution.py:401
  22.0 1.9 %collective-permute-start.1 = (f32[16,3328]{1,0:T(8,128)S(1)}, f32[16,3328]{1,0:T(8,128)S(1)}, u32[]{:S(2)}, u32[]{:S(2)}) collective-permute-start(f32[16,3328]{1,0:T(8,128)S(1)} %get-tuple-element.20), channel_id=1, source_target_pairs={{0,1},{1,2},{2,3},{3,4},{4,5},{5,6},{6,7},{7,8},{8,9},{9,10},{10,1... | collective-permute-start | bytes 638984 | tf_op jit(solution)/shard_map/ppermute | solution.py:553
  24.0 0.0 copy-start
  24.0 0.0 copy-start.1
  24.0 0.0 copy-start.2
  24.0 0.0 copy-start.5
  24.0 29.8 %tail.1.own = f32[16,8192]{1,0:T(8,128)S(1)} custom-call(s32[32]{0:T(128)S(1)} %copy-done.7, bf16[16,8704]{1,0:T(8,128)(2,1)S(1)} %get-tuple-element.13.refs_1_, f32[8,8704]{1,0:T(8,128)S(1)} %get-tuple-element.14.refs_2_, bf16[8448,48]{1,0:T(8,128)(2,1)S(1)} %get-tuple-element.15.refs_3_, f32[264,128]{1,0:T(8,128)S(1)} %get-tuple-element.16.refs_4_, ...), custom_call_target="tpu_custom_call" | custom-call | flops 10800000000 | bytes 4000000 | tf_op jit(solution)/shard_map/tail/pallas_call | solution.py:419
  53.9 0.0 copy-start.3
  53.9 0.0 copy-start.4
  53.9 0.0 copy-start.6
  53.9 0.0 collective-permute-done.1.back
  53.9 0.0 copy-done
  53.9 0.0 copy-done.1
  53.9 0.0 copy-done.2
  53.9 0.0 copy-done.5
  53.9 2.0 %sums.1 = (f32[16,8192]{1,0:T(8,128)S(1)}, f32[16,128]{1,0:T(8,128)S(1)}) custom-call(s32[32]{0:T(128)S(1)} %copy-done.7, f32[16,8192]{1,0:T(8,128)S(1)} %tail.1.own, f32[16,3328]{1,0:T(8,128)S(1)} %collective-permute-done.1.back, f32[1,8192]{1,0:T(1,128)S(1)} %bitcast.1, f32[16,8192]{1,0:T(8,128)S(1)} %copy-done, f32[16,8192]{1,0:T(8,128)S(1)} %copy-done.1, ...), custom_call_target="tpu_custom_call" | custom-call | tf_op jit(solution)/shard_map/sums/pallas_call | solution.py:478
  55.9 0.1 collective-permute-start.2
  56.0 1.2 %collective-permute-done.2 = f32[16,128]{1,0:T(8,128)S(1)} collective-permute-done((f32[16,128]{1,0:T(8,128)S(1)}, f32[16,128]{1,0:T(8,128)S(1)}, u32[]{:S(2)}, u32[]{:S(2)}) %collective-permute-start.2) | collective-permute-done | bytes 8224 | tf_op jit(solution)/shard_map/ppermute | solution.py:564
  57.2 10.5 %all_to_all.10 = f32[16,16,128]{2,1,0:T(8,128)S(1)} all-to-all(f32[16,16,128]{2,1,0:T(8,128)S(1)} %broadcast_in_dim.4), channel_id=1, replica_groups={{0,2,4,6,8,10,12,14,16,18,20,22,24,26,28,30},{1,3,5,7,9,11,13,15,17,19,..., dimensions={0} | all-to-all | bytes 262144 | tf_op jit(solution)/shard_map/all_to_all | solution.py:567
  67.7 16.2 %all_to_all.11 = f32[8,16,128]{2,1,0:T(8,128)S(1)} all-to-all(f32[8,16,128]{2,1,0:T(8,128)S(1)} %broadcast_in_dim.5), channel_id=1, replica_groups={{0,32,64,96,128,160,192,224},{1,33,65,97,129,161,193,225},{2,34,66,98,1..., dimensions={0} | all-to-all | bytes 131072 | tf_op jit(solution)/shard_map/all_to_all | solution.py:567
  83.9 0.0 copy-done.3
  83.9 0.0 copy-done.4
  83.9 0.0 copy-done.6
  83.9 2.3 %finish.1 = (f32[16,8192]{1,0:T(8,128)}, f32[16,8192]{1,0:T(8,128)}, f32[16,8192]{1,0:T(8,128)}) custom-call(s32[32]{0:T(128)S(1)} %copy-done.7, f32[16,128]{1,0:T(8,128)S(1)} %reduce_sum.19.sums, f32[32,32]{1,0:T(8,128)S(1)} %copy-done.6, f32[16,8192]{1,0:T(8,128)S(1)} %get-tuple-element.22.image, f32[16,8192]{1,0:T(8,128)S(1)} %copy-done, ...), custom_call_target="tpu_custom_call" | custom-call | tf_op jit(solution)/shard_map/finish/pallas_call | solution.py:539
  (5 shorter events, 0.1 us)
Async XLA Ops:
  1.7 10.3 %copy-start.7 = (s32[32]{0:T(128)S(1)}, s32[32]{0:T(128)}, u32[]{:S(2)}) copy-start(s32[32]{0:T(128)} %cnt.3) | copy-start | bytes 388
  1.7 10.3 %collective-permute-start = (f32[24,3072]{1,0:T(8,128)S(1)}, f32[24,3072]{1,0:T(8,128)S(1)}, u32[]{:S(2)}, u32[]{:S(2)}) collective-permute-start(f32[24,3072]{1,0:T(8,128)S(1)} %piece.1), channel_id=1, source_target_pairs={{1,0},{2,1},{3,2},{4,3},{5,4},{6,5},{7,6},{8,7},{9,8},{10,9},{11,1... | collective-permute-start | bytes 884744 | tf_op jit(solution)/shard_map/ppermute | solution.py:553
  22.0 31.9 %collective-permute-start.1 = (f32[16,3328]{1,0:T(8,128)S(1)}, f32[16,3328]{1,0:T(8,128)S(1)}, u32[]{:S(2)}, u32[]{:S(2)}) collective-permute-start(f32[16,3328]{1,0:T(8,128)S(1)} %get-tuple-element.20), channel_id=1, source_target_pairs={{0,1},{1,2},{2,3},{3,4},{4,5},{5,6},{6,7},{7,8},{8,9},{9,10},{10,1... | collective-permute-start | bytes 638984 | tf_op jit(solution)/shard_map/ppermute | solution.py:553
  24.0 29.9 %copy-start = (f32[16,8192]{1,0:T(8,128)S(1)}, f32[16,8192]{1,0:T(8,128)}, u32[]{:S(2)}) copy-start(f32[16,8192]{1,0:T(8,128)} %dirs.3) | copy-start | bytes 1572868
  24.0 29.9 %copy-start.1 = (f32[16,8192]{1,0:T(8,128)S(1)}, f32[16,8192]{1,0:T(8,128)}, u32[]{:S(2)}) copy-start(f32[16,8192]{1,0:T(8,128)} %res.3) | copy-start | bytes 1572868
  24.0 29.9 %copy-start.2 = (f32[32,8192]{1,0:T(8,128)S(1)}, f32[32,8192]{1,0:T(8,128)}, u32[]{:S(2)}) copy-start(f32[32,8192]{1,0:T(8,128)} %ritz.1) | copy-start | bytes 3145732
  24.0 29.9 %copy-start.5 = (f32[8192]{0:T(1024)S(1)}, f32[8192]{0:T(1024)}, u32[]{:S(2)}) copy-start(f32[8192]{0:T(1024)} %param.13) | copy-start | bytes 98308
  53.9 30.1 %copy-start.3 = (f32[32,8192]{1,0:T(8,128)S(1)}, f32[32,8192]{1,0:T(8,128)}, u32[]{:S(2)}) copy-start(f32[32,8192]{1,0:T(8,128)} %basis.1) | copy-start | bytes 3145732
  53.9 30.1 %copy-start.4 = (f32[16,8192]{1,0:T(8,128)S(1)}, f32[16,8192]{1,0:T(8,128)}, u32[]{:S(2)}) copy-start(f32[16,8192]{1,0:T(8,128)} %sol.1) | copy-start | bytes 1572868
  53.9 30.1 %copy-start.6 = (f32[32,32]{1,0:T(8,128)S(1)}, f32[32,32]{1,0:T(8,128)}, u32[]{:S(2)}) copy-start(f32[32,32]{1,0:T(8,128)} %gram.1) | copy-start | bytes 12292
  55.9 1.2 %collective-permute-start.2 = (f32[16,128]{1,0:T(8,128)S(1)}, f32[16,128]{1,0:T(8,128)S(1)}, u32[]{:S(2)}, u32[]{:S(2)}) collective-permute-start(f32[16,128]{1,0:T(8,128)S(1)} %get-tuple-element.21), channel_id=1, source_target_pairs={{0,1},{1,0},{2,3},{3,2},{4,5},{5,4},{6,7},{7,6},{8,9},{9,8},{10,11... | collective-permute-start | bytes 24584 | tf_op jit(solution)/shard_map/ppermute | solution.py:564
